TPU v7x, 128 devices: a whole 4x4x4 slice. The times are simulated.
128 devices in a mesh: shot: 16 (over z, x_hi, core), tile: 8 (over x_lo, y).
Axes of the slice: x: 4 (x_hi: 2, x_lo: 2; x = x_hi * 2 + x_lo), y: 4, z: 4, core: 2. Of those that a mesh axis runs over, the one named last changes fastest.
Arguments:
- lame_lambda: float32 [512, 32, 256], P(('shot', 'tile')), may hold values from 1 to 2
- lame_mu: float32 [512, 32, 256], P(('shot', 'tile')), may hold values from 0.5 to 1
- buoyancy: float32 [512, 32, 256], P(('shot', 'tile')), may hold values from 0.5 to 1
- aperture_row: int32 [16], replicated, may hold values from 0 to 15
- wave_state: float32 [16, 9, 32, 32, 256], P('shot', None, 'tile'), may hold values from -6 to 6
- source_cell: int32 [16], P('shot'), may hold values from 0 to 262143
- wavelet: float32 [16, 12], P('shot'), may hold values from -12 to 12
- receiver_cell: int32 [16, 256], P('shot'), may hold values from 0 to 262143
- prev_row: int32 [16], replicated, may hold values from 0 to 15
- prev_grad: float32 [16, 32, 32, 256], P('shot', 'tile'), may hold values from -6 to 6
Outputs:
- final_state: float32 [16, 9, 32, 32, 256], P('shot', None, 'tile')
- image_sum: float32 [16, 32, 32, 256], P('shot', 'tile')
- owner_grad: float32 [512, 32, 256], P(('shot', 'tile'))
- traces: float32 [16, 12, 256], P('shot')
Inputs may be any that keep to these rules, and one draw needn't show every extreme that they name: `aperture_row`: row q of model tiles holds the cells with x from q * 32 to q * 32 + 31; several shots may share a row and some rows have none. `prev_row`: rows of the previous batch, in the same sense. `source_cell`: flat index x * 32 * 256 + y * 256 + z within the shot's aperture. `receiver_cell`: flat indices as for source_cell; two receivers may share a cell.
All inputs are finite; a program needn't handle non-finite values.
Results may differ from a plain program's by a relative error of at most 0.0003.
Values sent between devices are 32-bit elements; how exact they have to be, the bound alone decides.
A program may use at most 64 MiB of HBM per device.

v0:
```python
import jax
import jax.numpy as jnp
from jax import lax
from jax.sharding import PartitionSpec as P

coefficients = (0.8, -0.2, 4.0 / 105.0, -1.0 / 280.0)
time_step = 0.2


def extended(cells, sides, width):
    for axis, dim in sides:
        count = lax.axis_size(axis)
        ends = count - 1
        head = lax.slice_in_dim(cells, 0, width, axis=dim)
        tail = lax.slice_in_dim(cells, cells.shape[dim] - width, cells.shape[dim], axis=dim)
        cells = jnp.concatenate(
            [
                lax.ppermute(tail, axis, [(i, (i + 1) % count) for i in range(ends)]),
                cells,
                lax.ppermute(head, axis, [((i + 1) % count, i) for i in range(ends)]),
            ],
            axis=dim,
        )
    return cells


def central(padded, axis, length):
    result = None
    for neighbor in range(1, 5):
        forward = lax.slice_in_dim(padded, 4 + neighbor, 4 + neighbor + length, axis=axis)
        backward = lax.slice_in_dim(padded, 4 - neighbor, 4 - neighbor + length, axis=axis)
        term = coefficients[neighbor - 1] * (forward - backward)
        result = term if result is None else result + term
    return result


def derive(field, axis):
    widths = [(0, 0)] * field.ndim
    widths[axis] = (4, 4)
    return central(jnp.pad(field, widths), axis, field.shape[axis])


def inject(velocity_z, buoy_cells, where_local, amplitude):
    flat = velocity_z.reshape(-1)
    count = flat.shape[0]
    inside = (where_local >= 0) & (where_local < count)
    index_at = jnp.clip(where_local, 0, count - 1)
    added = jnp.where(inside, time_step * buoy_cells.reshape(-1)[index_at] * amplitude, 0.0)
    return flat.at[index_at].add(added).reshape(velocity_z.shape)


def sample_at(velocity_z, where_local):
    flat = velocity_z.reshape(-1)
    count = flat.shape[0]
    inside = (where_local >= 0) & (where_local < count)
    index_at = jnp.clip(where_local, 0, count - 1)
    return jnp.where(inside, flat[index_at], 0.0)


def pad_stress(stacked):
    return extended(stacked, (("tile", 1),), 4)


def pad_velocity(stacked):
    return extended(stacked, (("tile", 1),), 4)


def advance_fields(fields, buoy_cells, lambda_cells, shear_cells, source_local, amplitude):
    (
        velocity_x,
        velocity_y,
        velocity_z,
        stress_xx,
        stress_yy,
        stress_zz,
        stress_xy,
        stress_xz,
        stress_yz,
    ) = fields
    length = velocity_x.shape[0]
    stress_dx = central(pad_stress(jnp.stack([stress_xx, stress_xy, stress_xz])), 1, length)
    velocity_x = velocity_x + time_step * buoy_cells * (
        stress_dx[0] + derive(stress_xy, 1) + derive(stress_xz, 2)
    )
    velocity_y = velocity_y + time_step * buoy_cells * (
        stress_dx[1] + derive(stress_yy, 1) + derive(stress_yz, 2)
    )
    velocity_z = velocity_z + time_step * buoy_cells * (
        stress_dx[2] + derive(stress_yz, 1) + derive(stress_zz, 2)
    )
    velocity_z = inject(velocity_z, buoy_cells, source_local, amplitude)
    velocity_dx = central(pad_velocity(jnp.stack([velocity_x, velocity_y, velocity_z])), 1, length)
    strain_xx = velocity_dx[0]
    strain_yy = derive(velocity_y, 1)
    strain_zz = derive(velocity_z, 2)
    dilation = strain_xx + strain_yy + strain_zz
    stress_xx = stress_xx + time_step * (lambda_cells * dilation + 2.0 * shear_cells * strain_xx)
    stress_yy = stress_yy + time_step * (lambda_cells * dilation + 2.0 * shear_cells * strain_yy)
    stress_zz = stress_zz + time_step * (lambda_cells * dilation + 2.0 * shear_cells * strain_zz)
    stress_xy = stress_xy + time_step * shear_cells * (derive(velocity_x, 1) + velocity_dx[1])
    stress_xz = stress_xz + time_step * shear_cells * (derive(velocity_x, 2) + velocity_dx[2])
    stress_yz = stress_yz + time_step * shear_cells * (
        derive(velocity_y, 2) + derive(velocity_z, 1)
    )
    increment = dilation * (stress_xx + stress_yy + stress_zz)
    fields = (
        velocity_x,
        velocity_y,
        velocity_z,
        stress_xx,
        stress_yy,
        stress_zz,
        stress_xy,
        stress_xz,
        stress_yz,
    )
    return (fields, increment)


def on_device(
    lame_lambda,
    lame_mu,
    buoyancy,
    aperture_row,
    wave_state,
    source_cell,
    wavelet,
    receiver_cell,
    prev_row,
    prev_grad,
):
    cells_x = lame_lambda.shape[0]
    shot_index = lax.axis_index("shot")
    tile_index = lax.axis_index("tile")
    my_row = aperture_row[shot_index]
    blank = (jnp.zeros_like(lame_lambda), jnp.zeros_like(lame_mu), jnp.zeros_like(buoyancy))
    pieces = (
        lax.all_gather(lame_lambda, "shot", axis=0, tiled=True),
        lax.all_gather(lame_mu, "shot", axis=0, tiled=True),
        lax.all_gather(buoyancy, "shot", axis=0, tiled=True),
    )
    offset = my_row * cells_x
    span = pieces[0].shape[0]
    inside = (offset >= 0) & (offset < span)
    begin = jnp.clip(offset, 0, span - cells_x)
    lambda_cells, shear_cells, buoy_cells = tuple(
        (
            jnp.where(inside, lax.dynamic_slice_in_dim(piece, begin, cells_x, 0), former)
            for piece, former in zip(pieces, blank)
        )
    )
    local_cells = cells_x * lame_lambda.shape[1] * lame_lambda.shape[2]
    first_cell = tile_index * local_cells
    source_local = source_cell[0] - first_cell
    receivers_local = receiver_cell[0] - first_cell
    state = wave_state[0]
    fields = tuple((state[index] for index in range(9)))

    def advance(carried, amplitude):
        fields, image_sum = carried
        fields, increment = advance_fields(
            fields, buoy_cells, lambda_cells, shear_cells, source_local, amplitude
        )
        record = sample_at(fields[2], receivers_local)
        record = lax.psum(record, "tile")
        return ((fields, image_sum + increment), record)

    (fields, image_sum), records = lax.scan(advance, (fields, jnp.zeros_like(state[0])), wavelet[0])
    grad_local = prev_grad[0]
    target = prev_row[shot_index]
    copies = cells_x * lax.axis_size("shot") // cells_x
    slot = jnp.arange(cells_x * lax.axis_size("shot"), dtype=jnp.int32) // cells_x
    owner_grad = lax.psum_scatter(
        jnp.where((slot == target)[:, None, None], jnp.tile(grad_local, (copies, 1, 1)), 0.0),
        "shot",
        scatter_dimension=0,
        tiled=True,
    )
    return (jnp.stack(fields)[None], image_sum[None], owner_grad, records[None])


def solution(mesh):
    placed = (
        P(("shot", "tile"), None, None),
        P(("shot", "tile"), None, None),
        P(("shot", "tile"), None, None),
        P(),
        P("shot", None, "tile", None, None),
        P("shot"),
        P("shot", None),
        P("shot", None),
        P(),
        P("shot", "tile", None, None),
    )
    return jax.shard_map(
        on_device,
        mesh=mesh,
        in_specs=placed,
        out_specs=(
            P("shot", None, "tile", None, None),
            P("shot", "tile", None, None),
            P(("shot", "tile"), None, None),
            P("shot", None, None),
        ),
        check_vma=False,
    )
```

profile of v0, /device:TPU:2, one launch (start us, length us, event | category | flops | bytes accessed | tf_op | source)
XLA Modules:
  0.0 700.0 jit_solution(10449325736466602303)
XLA Ops:
  17.0 42.5 %all-gather.4.cloned.1.call-done = f32[64,32,256]{2,1,0:T(8,128)} async-done(((f32[4,32,256]{2,1,0:T(8,128)}), f32[64,32,256]{2,1,0:T(8,128)}) %all-gather.4.cloned.1.call-update) | async-done | bytes 2097168 | tf_op jit(solution)/shard_map/all_gather | solution.py:140
  61.9 46.6 %all-gather.8.cloned.1.call-done = f32[64,32,256]{2,1,0:T(8,128)} async-done(((f32[4,32,256]{2,1,0:T(8,128)}), f32[64,32,256]{2,1,0:T(8,128)}) %all-gather.8.cloned.1.call-update) | async-done | bytes 2097168 | tf_op jit(solution)/shard_map/all_gather | solution.py:139
  109.4 48.0 %all-gather.6.cloned.1.call-done = f32[64,32,256]{2,1,0:T(8,128)} async-done(((f32[4,32,256]{2,1,0:T(8,128)}), f32[64,32,256]{2,1,0:T(8,128)}) %all-gather.6.cloned.1.call-update) | async-done | bytes 2097168 | tf_op jit(solution)/shard_map/all_gather | solution.py:138
  158.4 533.3 %while.34 = (s32[]{:T(128)}, f32[4,32,256]{2,1,0:T(8,128)S(1)}, f32[4,32,256]{2,1,0:T(8,128)S(1)}, f32[4,32,256]{2,1,0:T(8,128)S(1)}, f32[4,32,256]{2,1,0:T(8,12...) while((s32[]{:T(128)}, f32[4,32,256]{2,1,0:T(8,128)S(1)}, ...), condition=%wide.region_2.3_spmd.clone, body=%wide.region_0.2_spmd.clone.sunk | while | flops 10718471 | bytes 27152824 | solution.py:168
  158.4 5.5 collective-permute-start
  167.1 5.6 collective-permute-done
  172.7 6.2 collective-permute-done.1
  188.2 18.3 %psum.12 = f32[1,256]{1,0:T(1,128)S(1)} all-reduce(f32[1,256]{1,0:T(1,128)S(1)} %bitcast.139), channel_id=1, replica_groups=mesh['shot'=16,'tile'=8] {'tile'}, use_global_device_ids=true, to_apply=%region_1.1 | all-reduce | flops 256 | bytes 2048 | tf_op jit(solution)/shard_map/while/body/eval_jaxpr/psum | solution.py:165
  217.6 6.8 collective-permute-done.1
  233.8 18.1 %psum.12 = f32[1,256]{1,0:T(1,128)S(1)} all-reduce(f32[1,256]{1,0:T(1,128)S(1)} %bitcast.139), channel_id=1, replica_groups=mesh['shot'=16,'tile'=8] {'tile'}, use_global_device_ids=true, to_apply=%region_1.1 | all-reduce | flops 256 | bytes 2048 | tf_op jit(solution)/shard_map/while/body/eval_jaxpr/psum | solution.py:165
  277.3 18.1 %psum.12 = f32[1,256]{1,0:T(1,128)S(1)} all-reduce(f32[1,256]{1,0:T(1,128)S(1)} %bitcast.139), channel_id=1, replica_groups=mesh['shot'=16,'tile'=8] {'tile'}, use_global_device_ids=true, to_apply=%region_1.1 | all-reduce | flops 256 | bytes 2048 | tf_op jit(solution)/shard_map/while/body/eval_jaxpr/psum | solution.py:165
  304.0 4.6 collective-permute-done
  322.0 18.2 %psum.12 = f32[1,256]{1,0:T(1,128)S(1)} all-reduce(f32[1,256]{1,0:T(1,128)S(1)} %bitcast.139), channel_id=1, replica_groups=mesh['shot'=16,'tile'=8] {'tile'}, use_global_device_ids=true, to_apply=%region_1.1 | all-reduce | flops 256 | bytes 2048 | tf_op jit(solution)/shard_map/while/body/eval_jaxpr/psum | solution.py:165
  364.7 19.1 %psum.12 = f32[1,256]{1,0:T(1,128)S(1)} all-reduce(f32[1,256]{1,0:T(1,128)S(1)} %bitcast.139), channel_id=1, replica_groups=mesh['shot'=16,'tile'=8] {'tile'}, use_global_device_ids=true, to_apply=%region_1.1 | all-reduce | flops 256 | bytes 2048 | tf_op jit(solution)/shard_map/while/body/eval_jaxpr/psum | solution.py:165
  394.9 6.0 collective-permute-done.1
  410.2 18.2 %psum.12 = f32[1,256]{1,0:T(1,128)S(1)} all-reduce(f32[1,256]{1,0:T(1,128)S(1)} %bitcast.139), channel_id=1, replica_groups=mesh['shot'=16,'tile'=8] {'tile'}, use_global_device_ids=true, to_apply=%region_1.1 | all-reduce | flops 256 | bytes 2048 | tf_op jit(solution)/shard_map/while/body/eval_jaxpr/psum | solution.py:165
  452.8 18.2 %psum.12 = f32[1,256]{1,0:T(1,128)S(1)} all-reduce(f32[1,256]{1,0:T(1,128)S(1)} %bitcast.139), channel_id=1, replica_groups=mesh['shot'=16,'tile'=8] {'tile'}, use_global_device_ids=true, to_apply=%region_1.1 | all-reduce | flops 256 | bytes 2048 | tf_op jit(solution)/shard_map/while/body/eval_jaxpr/psum | solution.py:165
  496.9 18.1 %psum.12 = f32[1,256]{1,0:T(1,128)S(1)} all-reduce(f32[1,256]{1,0:T(1,128)S(1)} %bitcast.139), channel_id=1, replica_groups=mesh['shot'=16,'tile'=8] {'tile'}, use_global_device_ids=true, to_apply=%region_1.1 | all-reduce | flops 256 | bytes 2048 | tf_op jit(solution)/shard_map/while/body/eval_jaxpr/psum | solution.py:165
  523.5 4.5 collective-permute-done
  528.0 5.8 collective-permute-done.1
  543.1 18.1 %psum.12 = f32[1,256]{1,0:T(1,128)S(1)} all-reduce(f32[1,256]{1,0:T(1,128)S(1)} %bitcast.139), channel_id=1, replica_groups=mesh['shot'=16,'tile'=8] {'tile'}, use_global_device_ids=true, to_apply=%region_1.1 | all-reduce | flops 256 | bytes 2048 | tf_op jit(solution)/shard_map/while/body/eval_jaxpr/psum | solution.py:165
  586.0 18.1 %psum.12 = f32[1,256]{1,0:T(1,128)S(1)} all-reduce(f32[1,256]{1,0:T(1,128)S(1)} %bitcast.139), channel_id=1, replica_groups=mesh['shot'=16,'tile'=8] {'tile'}, use_global_device_ids=true, to_apply=%region_1.1 | all-reduce | flops 256 | bytes 2048 | tf_op jit(solution)/shard_map/while/body/eval_jaxpr/psum | solution.py:165
  629.5 18.1 %psum.12 = f32[1,256]{1,0:T(1,128)S(1)} all-reduce(f32[1,256]{1,0:T(1,128)S(1)} %bitcast.139), channel_id=1, replica_groups=mesh['shot'=16,'tile'=8] {'tile'}, use_global_device_ids=true, to_apply=%region_1.1 | all-reduce | flops 256 | bytes 2048 | tf_op jit(solution)/shard_map/while/body/eval_jaxpr/psum | solution.py:165
  672.1 18.1 %psum.12 = f32[1,256]{1,0:T(1,128)S(1)} all-reduce(f32[1,256]{1,0:T(1,128)S(1)} %bitcast.139), channel_id=1, replica_groups=mesh['shot'=16,'tile'=8] {'tile'}, use_global_device_ids=true, to_apply=%region_1.1 | all-reduce | flops 256 | bytes 2048 | tf_op jit(solution)/shard_map/while/body/eval_jaxpr/psum | solution.py:165
  (372 shorter events, 273.6 us)
Async XLA Ops:
  7.2 52.4 %all-gather.4.cloned.1.call-start = ((), (), s32[]{:S(2)}) async-start(), calls=%async_computation.1 | async-start | bytes 2228224 | tf_op jit(solution)/shard_map/all_gather | solution.py:140
  7.9 100.6 %all-gather.8.cloned.1.call-start = ((), (), s32[]{:S(2)}) async-start(), calls=%async_computation.3 | async-start | bytes 2228224 | tf_op jit(solution)/shard_map/all_gather | solution.py:139
  8.6 148.8 %all-gather.6.cloned.1.call-start = ((), (), s32[]{:S(2)}) async-start(), calls=%async_computation.2 | async-start | bytes 2228224 | tf_op jit(solution)/shard_map/all_gather | solution.py:138
  9.4 683.1 %reduce-scatter.2.cloned.1.call-start = ((), (), s32[]{:S(2)}) async-start(), calls=%async_computation.4 | async-start | bytes 2228224 | tf_op jit(solution)/shard_map/reduce_scatter | solution.py:173
  180.6 26.0 %collective-permute-start.2 = (f32[3,4,32,256]{3,2,1,0:T(8,128)S(1)}, f32[3,4,32,256]{3,2,1,0:T(8,128)S(1)}, u32[]{:S(2)}, u32[]{:S(2)}) collective-permute-start(f32[3,4,32,256]{3,2,1,0:T(8,128)S(1)} %pad_maximum_fusion.10), channel_id=1, source_target_pairs={{1,0},{2,1},{3,2},{4,3},{5,4},{6,5},{7,6},{9,8},{10,9},{11,10},{12... | collective-permute-start | bytes 1179656 | tf_op jit(solution)/shard_map/while/body/eval_jaxpr/ppermute | solution.py:20
  182.5 24.1 %collective-permute-start.3 = (f32[3,4,32,256]{3,2,1,0:T(8,128)S(1)}, f32[3,4,32,256]{3,2,1,0:T(8,128)S(1)}, u32[]{:S(2)}, u32[]{:S(2)}) collective-permute-start(f32[3,4,32,256]{3,2,1,0:T(8,128)S(1)} %pad_maximum_fusion.10), channel_id=1, source_target_pairs={{0,1},{1,2},{2,3},{3,4},{4,5},{5,6},{6,7},{8,9},{9,10},{10,11},{11... | collective-permute-start | bytes 1179656 | tf_op jit(solution)/shard_map/while/body/eval_jaxpr/ppermute | solution.py:18
  226.1 25.8 %collective-permute-start.2 = (f32[3,4,32,256]{3,2,1,0:T(8,128)S(1)}, f32[3,4,32,256]{3,2,1,0:T(8,128)S(1)}, u32[]{:S(2)}, u32[]{:S(2)}) collective-permute-start(f32[3,4,32,256]{3,2,1,0:T(8,128)S(1)} %pad_maximum_fusion.10), channel_id=1, source_target_pairs={{1,0},{2,1},{3,2},{4,3},{5,4},{6,5},{7,6},{9,8},{10,9},{11,10},{12... | collective-permute-start | bytes 1179656 | tf_op jit(solution)/shard_map/while/body/eval_jaxpr/ppermute | solution.py:20
  228.0 23.9 %collective-permute-start.3 = (f32[3,4,32,256]{3,2,1,0:T(8,128)S(1)}, f32[3,4,32,256]{3,2,1,0:T(8,128)S(1)}, u32[]{:S(2)}, u32[]{:S(2)}) collective-permute-start(f32[3,4,32,256]{3,2,1,0:T(8,128)S(1)} %pad_maximum_fusion.10), channel_id=1, source_target_pairs={{0,1},{1,2},{2,3},{3,4},{4,5},{5,6},{6,7},{8,9},{9,10},{10,11},{11... | collective-permute-start | bytes 1179656 | tf_op jit(solution)/shard_map/while/body/eval_jaxpr/ppermute | solution.py:18
  269.6 25.8 %collective-permute-start.2 = (f32[3,4,32,256]{3,2,1,0:T(8,128)S(1)}, f32[3,4,32,256]{3,2,1,0:T(8,128)S(1)}, u32[]{:S(2)}, u32[]{:S(2)}) collective-permute-start(f32[3,4,32,256]{3,2,1,0:T(8,128)S(1)} %pad_maximum_fusion.10), channel_id=1, source_target_pairs={{1,0},{2,1},{3,2},{4,3},{5,4},{6,5},{7,6},{9,8},{10,9},{11,10},{12... | collective-permute-start | bytes 1179656 | tf_op jit(solution)/shard_map/while/body/eval_jaxpr/ppermute | solution.py:20
  271.6 23.9 %collective-permute-start.3 = (f32[3,4,32,256]{3,2,1,0:T(8,128)S(1)}, f32[3,4,32,256]{3,2,1,0:T(8,128)S(1)}, u32[]{:S(2)}, u32[]{:S(2)}) collective-permute-start(f32[3,4,32,256]{3,2,1,0:T(8,128)S(1)} %pad_maximum_fusion.10), channel_id=1, source_target_pairs={{0,1},{1,2},{2,3},{3,4},{4,5},{5,6},{6,7},{8,9},{9,10},{10,11},{11... | collective-permute-start | bytes 1179656 | tf_op jit(solution)/shard_map/while/body/eval_jaxpr/ppermute | solution.py:18
  314.3 25.9 %collective-permute-start.2 = (f32[3,4,32,256]{3,2,1,0:T(8,128)S(1)}, f32[3,4,32,256]{3,2,1,0:T(8,128)S(1)}, u32[]{:S(2)}, u32[]{:S(2)}) collective-permute-start(f32[3,4,32,256]{3,2,1,0:T(8,128)S(1)} %pad_maximum_fusion.10), channel_id=1, source_target_pairs={{1,0},{2,1},{3,2},{4,3},{5,4},{6,5},{7,6},{9,8},{10,9},{11,10},{12... | collective-permute-start | bytes 1179656 | tf_op jit(solution)/shard_map/while/body/eval_jaxpr/ppermute | solution.py:20
  316.2 23.9 %collective-permute-start.3 = (f32[3,4,32,256]{3,2,1,0:T(8,128)S(1)}, f32[3,4,32,256]{3,2,1,0:T(8,128)S(1)}, u32[]{:S(2)}, u32[]{:S(2)}) collective-permute-start(f32[3,4,32,256]{3,2,1,0:T(8,128)S(1)} %pad_maximum_fusion.10), channel_id=1, source_target_pairs={{0,1},{1,2},{2,3},{3,4},{4,5},{5,6},{6,7},{8,9},{9,10},{10,11},{11... | collective-permute-start | bytes 1179656 | tf_op jit(solution)/shard_map/while/body/eval_jaxpr/ppermute | solution.py:18
  357.0 26.8 %collective-permute-start.2 = (f32[3,4,32,256]{3,2,1,0:T(8,128)S(1)}, f32[3,4,32,256]{3,2,1,0:T(8,128)S(1)}, u32[]{:S(2)}, u32[]{:S(2)}) collective-permute-start(f32[3,4,32,256]{3,2,1,0:T(8,128)S(1)} %pad_maximum_fusion.10), channel_id=1, source_target_pairs={{1,0},{2,1},{3,2},{4,3},{5,4},{6,5},{7,6},{9,8},{10,9},{11,10},{12... | collective-permute-start | bytes 1179656 | tf_op jit(solution)/shard_map/while/body/eval_jaxpr/ppermute | solution.py:20
  358.9 24.9 %collective-permute-start.3 = (f32[3,4,32,256]{3,2,1,0:T(8,128)S(1)}, f32[3,4,32,256]{3,2,1,0:T(8,128)S(1)}, u32[]{:S(2)}, u32[]{:S(2)}) collective-permute-start(f32[3,4,32,256]{3,2,1,0:T(8,128)S(1)} %pad_maximum_fusion.10), channel_id=1, source_target_pairs={{0,1},{1,2},{2,3},{3,4},{4,5},{5,6},{6,7},{8,9},{9,10},{10,11},{11... | collective-permute-start | bytes 1179656 | tf_op jit(solution)/shard_map/while/body/eval_jaxpr/ppermute | solution.py:18
  402.5 25.9 %collective-permute-start.2 = (f32[3,4,32,256]{3,2,1,0:T(8,128)S(1)}, f32[3,4,32,256]{3,2,1,0:T(8,128)S(1)}, u32[]{:S(2)}, u32[]{:S(2)}) collective-permute-start(f32[3,4,32,256]{3,2,1,0:T(8,128)S(1)} %pad_maximum_fusion.10), channel_id=1, source_target_pairs={{1,0},{2,1},{3,2},{4,3},{5,4},{6,5},{7,6},{9,8},{10,9},{11,10},{12... | collective-permute-start | bytes 1179656 | tf_op jit(solution)/shard_map/while/body/eval_jaxpr/ppermute | solution.py:20
  404.4 23.9 %collective-permute-start.3 = (f32[3,4,32,256]{3,2,1,0:T(8,128)S(1)}, f32[3,4,32,256]{3,2,1,0:T(8,128)S(1)}, u32[]{:S(2)}, u32[]{:S(2)}) collective-permute-start(f32[3,4,32,256]{3,2,1,0:T(8,128)S(1)} %pad_maximum_fusion.10), channel_id=1, source_target_pairs={{0,1},{1,2},{2,3},{3,4},{4,5},{5,6},{6,7},{8,9},{9,10},{10,11},{11... | collective-permute-start | bytes 1179656 | tf_op jit(solution)/shard_map/while/body/eval_jaxpr/ppermute | solution.py:18
  445.2 25.9 %collective-permute-start.2 = (f32[3,4,32,256]{3,2,1,0:T(8,128)S(1)}, f32[3,4,32,256]{3,2,1,0:T(8,128)S(1)}, u32[]{:S(2)}, u32[]{:S(2)}) collective-permute-start(f32[3,4,32,256]{3,2,1,0:T(8,128)S(1)} %pad_maximum_fusion.10), channel_id=1, source_target_pairs={{1,0},{2,1},{3,2},{4,3},{5,4},{6,5},{7,6},{9,8},{10,9},{11,10},{12... | collective-permute-start | bytes 1179656 | tf_op jit(solution)/shard_map/while/body/eval_jaxpr/ppermute | solution.py:20
  447.1 23.9 %collective-permute-start.3 = (f32[3,4,32,256]{3,2,1,0:T(8,128)S(1)}, f32[3,4,32,256]{3,2,1,0:T(8,128)S(1)}, u32[]{:S(2)}, u32[]{:S(2)}) collective-permute-start(f32[3,4,32,256]{3,2,1,0:T(8,128)S(1)} %pad_maximum_fusion.10), channel_id=1, source_target_pairs={{0,1},{1,2},{2,3},{3,4},{4,5},{5,6},{6,7},{8,9},{9,10},{10,11},{11... | collective-permute-start | bytes 1179656 | tf_op jit(solution)/shard_map/while/body/eval_jaxpr/ppermute | solution.py:18
  489.2 25.8 %collective-permute-start.2 = (f32[3,4,32,256]{3,2,1,0:T(8,128)S(1)}, f32[3,4,32,256]{3,2,1,0:T(8,128)S(1)}, u32[]{:S(2)}, u32[]{:S(2)}) collective-permute-start(f32[3,4,32,256]{3,2,1,0:T(8,128)S(1)} %pad_maximum_fusion.10), channel_id=1, source_target_pairs={{1,0},{2,1},{3,2},{4,3},{5,4},{6,5},{7,6},{9,8},{10,9},{11,10},{12... | collective-permute-start | bytes 1179656 | tf_op jit(solution)/shard_map/while/body/eval_jaxpr/ppermute | solution.py:20
  535.4 25.8 %collective-permute-start.2 = (f32[3,4,32,256]{3,2,1,0:T(8,128)S(1)}, f32[3,4,32,256]{3,2,1,0:T(8,128)S(1)}, u32[]{:S(2)}, u32[]{:S(2)}) collective-permute-start(f32[3,4,32,256]{3,2,1,0:T(8,128)S(1)} %pad_maximum_fusion.10), channel_id=1, source_target_pairs={{1,0},{2,1},{3,2},{4,3},{5,4},{6,5},{7,6},{9,8},{10,9},{11,10},{12... | collective-permute-start | bytes 1179656 | tf_op jit(solution)/shard_map/while/body/eval_jaxpr/ppermute | solution.py:20
  578.3 25.8 %collective-permute-start.2 = (f32[3,4,32,256]{3,2,1,0:T(8,128)S(1)}, f32[3,4,32,256]{3,2,1,0:T(8,128)S(1)}, u32[]{:S(2)}, u32[]{:S(2)}) collective-permute-start(f32[3,4,32,256]{3,2,1,0:T(8,128)S(1)} %pad_maximum_fusion.10), channel_id=1, source_target_pairs={{1,0},{2,1},{3,2},{4,3},{5,4},{6,5},{7,6},{9,8},{10,9},{11,10},{12... | collective-permute-start | bytes 1179656 | tf_op jit(solution)/shard_map/while/body/eval_jaxpr/ppermute | solution.py:20
  580.2 23.9 %collective-permute-start.3 = (f32[3,4,32,256]{3,2,1,0:T(8,128)S(1)}, f32[3,4,32,256]{3,2,1,0:T(8,128)S(1)}, u32[]{:S(2)}, u32[]{:S(2)}) collective-permute-start(f32[3,4,32,256]{3,2,1,0:T(8,128)S(1)} %pad_maximum_fusion.10), channel_id=1, source_target_pairs={{0,1},{1,2},{2,3},{3,4},{4,5},{5,6},{6,7},{8,9},{9,10},{10,11},{11... | collective-permute-start | bytes 1179656 | tf_op jit(solution)/shard_map/while/body/eval_jaxpr/ppermute | solution.py:18
  621.9 25.8 %collective-permute-start.2 = (f32[3,4,32,256]{3,2,1,0:T(8,128)S(1)}, f32[3,4,32,256]{3,2,1,0:T(8,128)S(1)}, u32[]{:S(2)}, u32[]{:S(2)}) collective-permute-start(f32[3,4,32,256]{3,2,1,0:T(8,128)S(1)} %pad_maximum_fusion.10), channel_id=1, source_target_pairs={{1,0},{2,1},{3,2},{4,3},{5,4},{6,5},{7,6},{9,8},{10,9},{11,10},{12... | collective-permute-start | bytes 1179656 | tf_op jit(solution)/shard_map/while/body/eval_jaxpr/ppermute | solution.py:20
  664.4 25.8 %collective-permute-start.2 = (f32[3,4,32,256]{3,2,1,0:T(8,128)S(1)}, f32[3,4,32,256]{3,2,1,0:T(8,128)S(1)}, u32[]{:S(2)}, u32[]{:S(2)}) collective-permute-start(f32[3,4,32,256]{3,2,1,0:T(8,128)S(1)} %pad_maximum_fusion.10), channel_id=1, source_target_pairs={{1,0},{2,1},{3,2},{4,3},{5,4},{6,5},{7,6},{9,8},{10,9},{11,10},{12... | collective-permute-start | bytes 1179656 | tf_op jit(solution)/shard_map/while/body/eval_jaxpr/ppermute | solution.py:20
  (34 other events, 525.0 us)
Sparse Core Ops, SparseCore 0:
  10.4 49.0 all-gather.3
  62.0 46.4 all-gather.7
  111.0 46.4 all-gather.5
  161.7 70.1 reduce-scatter.1
where the time goes:
time: 702 us; the launch traced here: 700 us
  waiting for transfers between devices  238 us (34%)
  blocking collectives  218 us (31%)
  starting transfers between devices  142 us (20%)
  other arithmetic  40.5 us (6%)
  local copies, waits for them, and re-layouts  35.4 us (5%)
  between operations  16 us (2%)
  loops' own time  10 us (1%)
    psum x12, blocking collectives, advance(): record = lax.psum(record, 'tile')  218 us
    ppermute x24, starting transfers between devices, extended(): lax.ppermute(tail, axis, [(i, (i + 1) % count) for i in range(ends)])  87 us
    ppermute x24, waiting for transfers between devices, extended(): lax.ppermute(tail, axis, [(i, (i + 1) % count) for i in range(ends)])  57.5 us
    ppermute x24, starting transfers between devices, extended(): lax.ppermute(head, axis, [((i + 1) % count, i) for i in range(ends)])  54.9 us
    all_gather x1, waiting for transfers between devices, on_device(): lax.all_gather(lame_lambda, 'shot', axis=0, tiled=True)  48 us
    all_gather x1, waiting for transfers between devices, on_device(): lax.all_gather(lame_mu, 'shot', axis=0, tiled=True)  46.6 us
    all_gather x1, waiting for transfers between devices, on_device(): lax.all_gather(buoyancy, 'shot', axis=0, tiled=True)  42.5 us
    ppermute x24, waiting for transfers between devices, extended(): lax.ppermute(head, axis, [((i + 1) % count, i) for i in range(ends)])  41.1 us
  transfers between devices with their start and end apart: 52, of which 27 were waited for; matrix products, arithmetic and copies ran while one was open for 11% of the time, Pallas kernels for 0%

commit v1 on v0

--- a/solution.py
+++ b/solution.py
@@ -162,7 +162,8 @@
             fields, buoy_cells, lambda_cells, shear_cells, source_local, amplitude
         )
         record = sample_at(fields[2], receivers_local)
-        record = lax.psum(record, "tile")
+        search_slot = lambda q_in: jnp.sum(jax.lax.all_gather(q_in, axis_name="tile"), axis=0)
+        record = search_slot(record)
         return ((fields, image_sum + increment), record)
 
     (fields, image_sum), records = lax.scan(advance, (fields, jnp.zeros_like(state[0])), wavelet[0])

time: 702 us -> 697 us (level)
  blocking collectives: 218 us -> 210 us
    psum x12 -> x0, blocking collectives: 218 us -> none  [advance(): record = lax.psum(record, 'tile')]
    all_gather x0 -> x12, blocking collectives: none -> 210 us  [advance(): jax.lax.all_gather(q_in, axis_name='tile')]
where the time goes in v1:
time: 697 us; the launch traced here: 696 us
  waiting for transfers between devices  241 us (35%)
  blocking collectives  210 us (30%)
  starting transfers between devices  142 us (20%)
  other arithmetic  40.8 us (6%)
  local copies, waits for them, and re-layouts  35.5 us (5%)
  between operations  16 us (2%)
  loops' own time  10.1 us (1%)
    all_gather x12, blocking collectives, advance(): jax.lax.all_gather(q_in, axis_name='tile')  210 us
    ppermute x24, starting transfers between devices, extended(): lax.ppermute(tail, axis, [(i, (i + 1) % count) for i in range(ends)])  86.2 us
    ppermute x24, waiting for transfers between devices, extended(): lax.ppermute(tail, axis, [(i, (i + 1) % count) for i in range(ends)])  57.5 us
    ppermute x24, starting transfers between devices, extended(): lax.ppermute(head, axis, [((i + 1) % count, i) for i in range(ends)])  56 us
    all_gather x1, waiting for transfers between devices, on_device(): lax.all_gather(lame_lambda, 'shot', axis=0, tiled=True)  48 us
    all_gather x1, waiting for transfers between devices, on_device(): lax.all_gather(lame_mu, 'shot', axis=0, tiled=True)  46.6 us
    ppermute x24, waiting for transfers between devices, extended(): lax.ppermute(head, axis, [((i + 1) % count, i) for i in range(ends)])  44 us
    all_gather x1, waiting for transfers between devices, on_device(): lax.all_gather(buoyancy, 'shot', axis=0, tiled=True)  42.5 us
  transfers between devices with their start and end apart: 52, of which 27 were waited for; matrix products, arithmetic and copies ran while one was open for 11% of the time, Pallas kernels for 0%

profile of v1, /device:TPU:2, one launch (start us, length us, event | category | flops | bytes accessed | tf_op | source)
XLA Modules:
  0.0 695.5 jit_solution(10302262534648870560)
XLA Ops:
  17.0 42.5 %all-gather.9.cloned.1.call-done = f32[64,32,256]{2,1,0:T(8,128)} async-done(((f32[4,32,256]{2,1,0:T(8,128)}), f32[64,32,256]{2,1,0:T(8,128)}) %all-gather.9.cloned.1.call-update) | async-done | bytes 2097168 | tf_op jit(solution)/shard_map/all_gather | solution.py:140
  61.9 46.6 %all-gather.13.cloned.1.call-done = f32[64,32,256]{2,1,0:T(8,128)} async-done(((f32[4,32,256]{2,1,0:T(8,128)}), f32[64,32,256]{2,1,0:T(8,128)}) %all-gather.13.cloned.1.call-update) | async-done | bytes 2097168 | tf_op jit(solution)/shard_map/all_gather | solution.py:139
  109.4 48.0 %all-gather.11.cloned.1.call-done = f32[64,32,256]{2,1,0:T(8,128)} async-done(((f32[4,32,256]{2,1,0:T(8,128)}), f32[64,32,256]{2,1,0:T(8,128)}) %all-gather.11.cloned.1.call-update) | async-done | bytes 2097168 | tf_op jit(solution)/shard_map/all_gather | solution.py:138
  158.4 528.8 %while.34 = (s32[]{:T(128)}, f32[4,32,256]{2,1,0:T(8,128)S(1)}, f32[4,32,256]{2,1,0:T(8,128)S(1)}, f32[4,32,256]{2,1,0:T(8,128)S(1)}, f32[4,32,256]{2,1,0:T(8,12...) while((s32[]{:T(128)}, f32[4,32,256]{2,1,0:T(8,128)S(1)}, ...), condition=%wide.region_2.3_spmd.clone, body=%wide.region_0.2_spmd.clone.sunk | while | flops 10720007 | bytes 27169212 | solution.py:169
  158.4 5.5 collective-permute-start
  167.1 5.6 collective-permute-done
  172.7 6.2 collective-permute-done.1
  188.2 17.3 %all-gather.4 = f32[8,1,256]{2,1,0:T(1,128)S(1)} all-gather(f32[1,1,256]{2,1,0:T(1,128)S(1)} %bitcast.142), channel_id=2, replica_groups=mesh['shot'=16,'tile'=8] {'tile'}, dimensions={0}, use_global_device_ids=true | all-gather | bytes 9216 | tf_op jit(solution)/shard_map/while/body/eval_jaxpr/all_gather | solution.py:165
  216.8 7.4 %collective-permute-done.1 = f32[3,4,32,256]{3,2,1,0:T(8,128)S(1)} collective-permute-done((f32[3,4,32,256]{3,2,1,0:T(8,128)S(1)}, f32[3,4,32,256]{3,2,1,0:T(8,128)S(1)}, u32[]{:S(2)}, u32[]{:S(2)}) %collective-permute-start.1) | collective-permute-done | bytes 393248 | tf_op jit(solution)/shard_map/while/body/eval_jaxpr/ppermute | solution.py:18
  233.5 17.2 %all-gather.4 = f32[8,1,256]{2,1,0:T(1,128)S(1)} all-gather(f32[1,1,256]{2,1,0:T(1,128)S(1)} %bitcast.142), channel_id=2, replica_groups=mesh['shot'=16,'tile'=8] {'tile'}, dimensions={0}, use_global_device_ids=true | all-gather | bytes 9216 | tf_op jit(solution)/shard_map/while/body/eval_jaxpr/all_gather | solution.py:165
  276.7 17.2 %all-gather.4 = f32[8,1,256]{2,1,0:T(1,128)S(1)} all-gather(f32[1,1,256]{2,1,0:T(1,128)S(1)} %bitcast.142), channel_id=2, replica_groups=mesh['shot'=16,'tile'=8] {'tile'}, dimensions={0}, use_global_device_ids=true | all-gather | bytes 9216 | tf_op jit(solution)/shard_map/while/body/eval_jaxpr/all_gather | solution.py:165
  320.6 17.2 %all-gather.4 = f32[8,1,256]{2,1,0:T(1,128)S(1)} all-gather(f32[1,1,256]{2,1,0:T(1,128)S(1)} %bitcast.142), channel_id=2, replica_groups=mesh['shot'=16,'tile'=8] {'tile'}, dimensions={0}, use_global_device_ids=true | all-gather | bytes 9216 | tf_op jit(solution)/shard_map/while/body/eval_jaxpr/all_gather | solution.py:165
  362.4 18.8 %all-gather.4 = f32[8,1,256]{2,1,0:T(1,128)S(1)} all-gather(f32[1,1,256]{2,1,0:T(1,128)S(1)} %bitcast.142), channel_id=2, replica_groups=mesh['shot'=16,'tile'=8] {'tile'}, dimensions={0}, use_global_device_ids=true | all-gather | bytes 9216 | tf_op jit(solution)/shard_map/while/body/eval_jaxpr/all_gather | solution.py:165
  392.6 6.0 collective-permute-done.1
  407.9 17.2 %all-gather.4 = f32[8,1,256]{2,1,0:T(1,128)S(1)} all-gather(f32[1,1,256]{2,1,0:T(1,128)S(1)} %bitcast.142), channel_id=2, replica_groups=mesh['shot'=16,'tile'=8] {'tile'}, dimensions={0}, use_global_device_ids=true | all-gather | bytes 9216 | tf_op jit(solution)/shard_map/while/body/eval_jaxpr/all_gather | solution.py:165
  449.7 17.2 %all-gather.4 = f32[8,1,256]{2,1,0:T(1,128)S(1)} all-gather(f32[1,1,256]{2,1,0:T(1,128)S(1)} %bitcast.142), channel_id=2, replica_groups=mesh['shot'=16,'tile'=8] {'tile'}, dimensions={0}, use_global_device_ids=true | all-gather | bytes 9216 | tf_op jit(solution)/shard_map/while/body/eval_jaxpr/all_gather | solution.py:165
  475.6 5.4 collective-permute-done
  494.3 18.9 %all-gather.4 = f32[8,1,256]{2,1,0:T(1,128)S(1)} all-gather(f32[1,1,256]{2,1,0:T(1,128)S(1)} %bitcast.142), channel_id=2, replica_groups=mesh['shot'=16,'tile'=8] {'tile'}, dimensions={0}, use_global_device_ids=true | all-gather | bytes 9216 | tf_op jit(solution)/shard_map/while/body/eval_jaxpr/all_gather | solution.py:165
  525.4 5.5 collective-permute-done.1
  540.2 17.2 %all-gather.4 = f32[8,1,256]{2,1,0:T(1,128)S(1)} all-gather(f32[1,1,256]{2,1,0:T(1,128)S(1)} %bitcast.142), channel_id=2, replica_groups=mesh['shot'=16,'tile'=8] {'tile'}, dimensions={0}, use_global_device_ids=true | all-gather | bytes 9216 | tf_op jit(solution)/shard_map/while/body/eval_jaxpr/all_gather | solution.py:165
  581.9 17.2 %all-gather.4 = f32[8,1,256]{2,1,0:T(1,128)S(1)} all-gather(f32[1,1,256]{2,1,0:T(1,128)S(1)} %bitcast.142), channel_id=2, replica_groups=mesh['shot'=16,'tile'=8] {'tile'}, dimensions={0}, use_global_device_ids=true | all-gather | bytes 9216 | tf_op jit(solution)/shard_map/while/body/eval_jaxpr/all_gather | solution.py:165
  607.8 5.6 collective-permute-done
  626.7 17.2 %all-gather.4 = f32[8,1,256]{2,1,0:T(1,128)S(1)} all-gather(f32[1,1,256]{2,1,0:T(1,128)S(1)} %bitcast.142), channel_id=2, replica_groups=mesh['shot'=16,'tile'=8] {'tile'}, dimensions={0}, use_global_device_ids=true | all-gather | bytes 9216 | tf_op jit(solution)/shard_map/while/body/eval_jaxpr/all_gather | solution.py:165
  668.5 17.2 %all-gather.4 = f32[8,1,256]{2,1,0:T(1,128)S(1)} all-gather(f32[1,1,256]{2,1,0:T(1,128)S(1)} %bitcast.142), channel_id=2, replica_groups=mesh['shot'=16,'tile'=8] {'tile'}, dimensions={0}, use_global_device_ids=true | all-gather | bytes 9216 | tf_op jit(solution)/shard_map/while/body/eval_jaxpr/all_gather | solution.py:165
  (384 shorter events, 275.0 us)
Async XLA Ops:
  7.2 52.4 %all-gather.9.cloned.1.call-start = ((), (), s32[]{:S(2)}) async-start(), calls=%async_computation.1 | async-start | bytes 2228224 | tf_op jit(solution)/shard_map/all_gather | solution.py:140
  7.9 100.6 %all-gather.13.cloned.1.call-start = ((), (), s32[]{:S(2)}) async-start(), calls=%async_computation.3 | async-start | bytes 2228224 | tf_op jit(solution)/shard_map/all_gather | solution.py:139
  8.6 148.8 %all-gather.11.cloned.1.call-start = ((), (), s32[]{:S(2)}) async-start(), calls=%async_computation.2 | async-start | bytes 2228224 | tf_op jit(solution)/shard_map/all_gather | solution.py:138
  9.4 678.6 %reduce-scatter.2.cloned.1.call-start = ((), (), s32[]{:S(2)}) async-start(), calls=%async_computation.4 | async-start | bytes 2228224 | tf_op jit(solution)/shard_map/reduce_scatter | solution.py:174
  180.6 25.1 %collective-permute-start.2 = (f32[3,4,32,256]{3,2,1,0:T(8,128)S(1)}, f32[3,4,32,256]{3,2,1,0:T(8,128)S(1)}, u32[]{:S(2)}, u32[]{:S(2)}) collective-permute-start(f32[3,4,32,256]{3,2,1,0:T(8,128)S(1)} %pad_maximum_fusion.10), channel_id=1, source_target_pairs={{1,0},{2,1},{3,2},{4,3},{5,4},{6,5},{7,6},{9,8},{10,9},{11,10},{12... | collective-permute-start | bytes 1179656 | tf_op jit(solution)/shard_map/while/body/eval_jaxpr/ppermute | solution.py:20
  182.5 23.1 %collective-permute-start.3 = (f32[3,4,32,256]{3,2,1,0:T(8,128)S(1)}, f32[3,4,32,256]{3,2,1,0:T(8,128)S(1)}, u32[]{:S(2)}, u32[]{:S(2)}) collective-permute-start(f32[3,4,32,256]{3,2,1,0:T(8,128)S(1)} %pad_maximum_fusion.10), channel_id=1, source_target_pairs={{0,1},{1,2},{2,3},{3,4},{4,5},{5,6},{6,7},{8,9},{9,10},{10,11},{11... | collective-permute-start | bytes 1179656 | tf_op jit(solution)/shard_map/while/body/eval_jaxpr/ppermute | solution.py:18
  225.9 25.0 %collective-permute-start.2 = (f32[3,4,32,256]{3,2,1,0:T(8,128)S(1)}, f32[3,4,32,256]{3,2,1,0:T(8,128)S(1)}, u32[]{:S(2)}, u32[]{:S(2)}) collective-permute-start(f32[3,4,32,256]{3,2,1,0:T(8,128)S(1)} %pad_maximum_fusion.10), channel_id=1, source_target_pairs={{1,0},{2,1},{3,2},{4,3},{5,4},{6,5},{7,6},{9,8},{10,9},{11,10},{12... | collective-permute-start | bytes 1179656 | tf_op jit(solution)/shard_map/while/body/eval_jaxpr/ppermute | solution.py:20
  227.8 23.1 %collective-permute-start.3 = (f32[3,4,32,256]{3,2,1,0:T(8,128)S(1)}, f32[3,4,32,256]{3,2,1,0:T(8,128)S(1)}, u32[]{:S(2)}, u32[]{:S(2)}) collective-permute-start(f32[3,4,32,256]{3,2,1,0:T(8,128)S(1)} %pad_maximum_fusion.10), channel_id=1, source_target_pairs={{0,1},{1,2},{2,3},{3,4},{4,5},{5,6},{6,7},{8,9},{9,10},{10,11},{11... | collective-permute-start | bytes 1179656 | tf_op jit(solution)/shard_map/while/body/eval_jaxpr/ppermute | solution.py:18
  269.0 25.0 %collective-permute-start.2 = (f32[3,4,32,256]{3,2,1,0:T(8,128)S(1)}, f32[3,4,32,256]{3,2,1,0:T(8,128)S(1)}, u32[]{:S(2)}, u32[]{:S(2)}) collective-permute-start(f32[3,4,32,256]{3,2,1,0:T(8,128)S(1)} %pad_maximum_fusion.10), channel_id=1, source_target_pairs={{1,0},{2,1},{3,2},{4,3},{5,4},{6,5},{7,6},{9,8},{10,9},{11,10},{12... | collective-permute-start | bytes 1179656 | tf_op jit(solution)/shard_map/while/body/eval_jaxpr/ppermute | solution.py:20
  270.9 23.1 %collective-permute-start.3 = (f32[3,4,32,256]{3,2,1,0:T(8,128)S(1)}, f32[3,4,32,256]{3,2,1,0:T(8,128)S(1)}, u32[]{:S(2)}, u32[]{:S(2)}) collective-permute-start(f32[3,4,32,256]{3,2,1,0:T(8,128)S(1)} %pad_maximum_fusion.10), channel_id=1, source_target_pairs={{0,1},{1,2},{2,3},{3,4},{4,5},{5,6},{6,7},{8,9},{9,10},{10,11},{11... | collective-permute-start | bytes 1179656 | tf_op jit(solution)/shard_map/while/body/eval_jaxpr/ppermute | solution.py:18
  312.9 25.0 %collective-permute-start.2 = (f32[3,4,32,256]{3,2,1,0:T(8,128)S(1)}, f32[3,4,32,256]{3,2,1,0:T(8,128)S(1)}, u32[]{:S(2)}, u32[]{:S(2)}) collective-permute-start(f32[3,4,32,256]{3,2,1,0:T(8,128)S(1)} %pad_maximum_fusion.10), channel_id=1, source_target_pairs={{1,0},{2,1},{3,2},{4,3},{5,4},{6,5},{7,6},{9,8},{10,9},{11,10},{12... | collective-permute-start | bytes 1179656 | tf_op jit(solution)/shard_map/while/body/eval_jaxpr/ppermute | solution.py:20
  314.8 23.1 %collective-permute-start.3 = (f32[3,4,32,256]{3,2,1,0:T(8,128)S(1)}, f32[3,4,32,256]{3,2,1,0:T(8,128)S(1)}, u32[]{:S(2)}, u32[]{:S(2)}) collective-permute-start(f32[3,4,32,256]{3,2,1,0:T(8,128)S(1)} %pad_maximum_fusion.10), channel_id=1, source_target_pairs={{0,1},{1,2},{2,3},{3,4},{4,5},{5,6},{6,7},{8,9},{9,10},{10,11},{11... | collective-permute-start | bytes 1179656 | tf_op jit(solution)/shard_map/while/body/eval_jaxpr/ppermute | solution.py:18
  354.7 26.5 %collective-permute-start.2 = (f32[3,4,32,256]{3,2,1,0:T(8,128)S(1)}, f32[3,4,32,256]{3,2,1,0:T(8,128)S(1)}, u32[]{:S(2)}, u32[]{:S(2)}) collective-permute-start(f32[3,4,32,256]{3,2,1,0:T(8,128)S(1)} %pad_maximum_fusion.10), channel_id=1, source_target_pairs={{1,0},{2,1},{3,2},{4,3},{5,4},{6,5},{7,6},{9,8},{10,9},{11,10},{12... | collective-permute-start | bytes 1179656 | tf_op jit(solution)/shard_map/while/body/eval_jaxpr/ppermute | solution.py:20
  356.6 24.6 %collective-permute-start.3 = (f32[3,4,32,256]{3,2,1,0:T(8,128)S(1)}, f32[3,4,32,256]{3,2,1,0:T(8,128)S(1)}, u32[]{:S(2)}, u32[]{:S(2)}) collective-permute-start(f32[3,4,32,256]{3,2,1,0:T(8,128)S(1)} %pad_maximum_fusion.10), channel_id=1, source_target_pairs={{0,1},{1,2},{2,3},{3,4},{4,5},{5,6},{6,7},{8,9},{9,10},{10,11},{11... | collective-permute-start | bytes 1179656 | tf_op jit(solution)/shard_map/while/body/eval_jaxpr/ppermute | solution.py:18
  400.3 25.0 %collective-permute-start.2 = (f32[3,4,32,256]{3,2,1,0:T(8,128)S(1)}, f32[3,4,32,256]{3,2,1,0:T(8,128)S(1)}, u32[]{:S(2)}, u32[]{:S(2)}) collective-permute-start(f32[3,4,32,256]{3,2,1,0:T(8,128)S(1)} %pad_maximum_fusion.10), channel_id=1, source_target_pairs={{1,0},{2,1},{3,2},{4,3},{5,4},{6,5},{7,6},{9,8},{10,9},{11,10},{12... | collective-permute-start | bytes 1179656 | tf_op jit(solution)/shard_map/while/body/eval_jaxpr/ppermute | solution.py:20
  442.0 25.0 %collective-permute-start.2 = (f32[3,4,32,256]{3,2,1,0:T(8,128)S(1)}, f32[3,4,32,256]{3,2,1,0:T(8,128)S(1)}, u32[]{:S(2)}, u32[]{:S(2)}) collective-permute-start(f32[3,4,32,256]{3,2,1,0:T(8,128)S(1)} %pad_maximum_fusion.10), channel_id=1, source_target_pairs={{1,0},{2,1},{3,2},{4,3},{5,4},{6,5},{7,6},{9,8},{10,9},{11,10},{12... | collective-permute-start | bytes 1179656 | tf_op jit(solution)/shard_map/while/body/eval_jaxpr/ppermute | solution.py:20
  444.0 23.1 %collective-permute-start.3 = (f32[3,4,32,256]{3,2,1,0:T(8,128)S(1)}, f32[3,4,32,256]{3,2,1,0:T(8,128)S(1)}, u32[]{:S(2)}, u32[]{:S(2)}) collective-permute-start(f32[3,4,32,256]{3,2,1,0:T(8,128)S(1)} %pad_maximum_fusion.10), channel_id=1, source_target_pairs={{0,1},{1,2},{2,3},{3,4},{4,5},{5,6},{6,7},{8,9},{9,10},{10,11},{11... | collective-permute-start | bytes 1179656 | tf_op jit(solution)/shard_map/while/body/eval_jaxpr/ppermute | solution.py:18
  486.6 26.7 %collective-permute-start.2 = (f32[3,4,32,256]{3,2,1,0:T(8,128)S(1)}, f32[3,4,32,256]{3,2,1,0:T(8,128)S(1)}, u32[]{:S(2)}, u32[]{:S(2)}) collective-permute-start(f32[3,4,32,256]{3,2,1,0:T(8,128)S(1)} %pad_maximum_fusion.10), channel_id=1, source_target_pairs={{1,0},{2,1},{3,2},{4,3},{5,4},{6,5},{7,6},{9,8},{10,9},{11,10},{12... | collective-permute-start | bytes 1179656 | tf_op jit(solution)/shard_map/while/body/eval_jaxpr/ppermute | solution.py:20
  488.6 24.8 %collective-permute-start.3 = (f32[3,4,32,256]{3,2,1,0:T(8,128)S(1)}, f32[3,4,32,256]{3,2,1,0:T(8,128)S(1)}, u32[]{:S(2)}, u32[]{:S(2)}) collective-permute-start(f32[3,4,32,256]{3,2,1,0:T(8,128)S(1)} %pad_maximum_fusion.10), channel_id=1, source_target_pairs={{0,1},{1,2},{2,3},{3,4},{4,5},{5,6},{6,7},{8,9},{9,10},{10,11},{11... | collective-permute-start | bytes 1179656 | tf_op jit(solution)/shard_map/while/body/eval_jaxpr/ppermute | solution.py:18
  532.5 25.0 %collective-permute-start.2 = (f32[3,4,32,256]{3,2,1,0:T(8,128)S(1)}, f32[3,4,32,256]{3,2,1,0:T(8,128)S(1)}, u32[]{:S(2)}, u32[]{:S(2)}) collective-permute-start(f32[3,4,32,256]{3,2,1,0:T(8,128)S(1)} %pad_maximum_fusion.10), channel_id=1, source_target_pairs={{1,0},{2,1},{3,2},{4,3},{5,4},{6,5},{7,6},{9,8},{10,9},{11,10},{12... | collective-permute-start | bytes 1179656 | tf_op jit(solution)/shard_map/while/body/eval_jaxpr/ppermute | solution.py:20
  574.2 25.0 %collective-permute-start.2 = (f32[3,4,32,256]{3,2,1,0:T(8,128)S(1)}, f32[3,4,32,256]{3,2,1,0:T(8,128)S(1)}, u32[]{:S(2)}, u32[]{:S(2)}) collective-permute-start(f32[3,4,32,256]{3,2,1,0:T(8,128)S(1)} %pad_maximum_fusion.10), channel_id=1, source_target_pairs={{1,0},{2,1},{3,2},{4,3},{5,4},{6,5},{7,6},{9,8},{10,9},{11,10},{12... | collective-permute-start | bytes 1179656 | tf_op jit(solution)/shard_map/while/body/eval_jaxpr/ppermute | solution.py:20
  576.2 23.1 %collective-permute-start.3 = (f32[3,4,32,256]{3,2,1,0:T(8,128)S(1)}, f32[3,4,32,256]{3,2,1,0:T(8,128)S(1)}, u32[]{:S(2)}, u32[]{:S(2)}) collective-permute-start(f32[3,4,32,256]{3,2,1,0:T(8,128)S(1)} %pad_maximum_fusion.10), channel_id=1, source_target_pairs={{0,1},{1,2},{2,3},{3,4},{4,5},{5,6},{6,7},{8,9},{9,10},{10,11},{11... | collective-permute-start | bytes 1179656 | tf_op jit(solution)/shard_map/while/body/eval_jaxpr/ppermute | solution.py:18
  619.0 25.0 %collective-permute-start.2 = (f32[3,4,32,256]{3,2,1,0:T(8,128)S(1)}, f32[3,4,32,256]{3,2,1,0:T(8,128)S(1)}, u32[]{:S(2)}, u32[]{:S(2)}) collective-permute-start(f32[3,4,32,256]{3,2,1,0:T(8,128)S(1)} %pad_maximum_fusion.10), channel_id=1, source_target_pairs={{1,0},{2,1},{3,2},{4,3},{5,4},{6,5},{7,6},{9,8},{10,9},{11,10},{12... | collective-permute-start | bytes 1179656 | tf_op jit(solution)/shard_map/while/body/eval_jaxpr/ppermute | solution.py:20
  660.8 25.0 %collective-permute-start.2 = (f32[3,4,32,256]{3,2,1,0:T(8,128)S(1)}, f32[3,4,32,256]{3,2,1,0:T(8,128)S(1)}, u32[]{:S(2)}, u32[]{:S(2)}) collective-permute-start(f32[3,4,32,256]{3,2,1,0:T(8,128)S(1)} %pad_maximum_fusion.10), channel_id=1, source_target_pairs={{1,0},{2,1},{3,2},{4,3},{5,4},{6,5},{7,6},{9,8},{10,9},{11,10},{12... | collective-permute-start | bytes 1179656 | tf_op jit(solution)/shard_map/while/body/eval_jaxpr/ppermute | solution.py:20
  (34 other events, 527.1 us)
Sparse Core Ops, SparseCore 0:
  10.4 49.0 all-gather.8
  62.0 46.4 all-gather.12
  111.0 46.4 all-gather.10
  161.7 70.1 reduce-scatter.1
